TPU v7x, 32 devices: a whole 2x2x4 slice. The times are simulated.
32 devices in a mesh: dp: 2 (over x), ctx: 4 (over y, core), tp: 4 (over z).
Axes of the slice: x: 2, y: 2, z: 4, core: 2. Of those that a mesh axis runs over, the one named last changes fastest.
Arguments:
- tokens: bfloat16 [16384, 768], P(('dp', 'ctx', 'tp')), may hold values from -6 to 6
- first_gain: bfloat16 [768], replicated, may hold values from 0.5 to 1.5
- first_bias: bfloat16 [768], replicated, may hold values from -0.4375 to 0.4375
- mixer_weight: bfloat16 [768, 3, 768], P(None, None, 'tp'), may hold values from -0.21875 to 0.21875
- mixer_bias: bfloat16 [3, 768], P(None, 'tp'), may hold values from -0.3125 to 0.3125
- feature_weight: bfloat16 [2, 12, 64, 64], P(None, 'tp'), may hold values from -1.5 to 1.5
- feature_bias: bfloat16 [2, 12, 64], P(None, 'tp'), may hold values from -6 to 6
- output_weight: bfloat16 [768, 768], P('tp'), may hold values from -6 to 6
- output_bias: bfloat16 [768], replicated, may hold values from -4 to 4
- second_gain: bfloat16 [768], replicated, may hold values from 0.5 to 1.5
- second_bias: bfloat16 [768], replicated, may hold values from -4 to 4
- inner_weight: bfloat16 [768, 3072], P(None, 'tp'), may hold values from -0.21875 to 0.21875
- inner_bias: bfloat16 [3072], P('tp'), may hold values from -4 to 4
- outer_weight: bfloat16 [3072, 768], P('tp'), may hold values from -0.109375 to 0.109375
- outer_bias: bfloat16 [768], replicated, may hold values from -4 to 4
- block_owner: int32 [2, 32], P('dp'), may hold values from 0 to 0, as said below
- cotangent: bfloat16 [16384, 768], P(('dp', 'ctx', 'tp')), may hold values from -6 to 6
Outputs:
- result: bfloat16 [16384, 768], P(('dp', 'ctx', 'tp'))
- tokens_gradient: float32 [16384, 768], P(('dp', 'ctx', 'tp'))
- first_gain_gradient: float32 [768], replicated
- first_bias_gradient: float32 [768], replicated
- mixer_weight_gradient: float32 [768, 3, 768], P(None, None, 'tp')
- mixer_bias_gradient: float32 [3, 768], P(None, 'tp')
- feature_weight_gradient: float32 [2, 12, 64, 64], P(None, 'tp')
- feature_bias_gradient: float32 [2, 12, 64], P(None, 'tp')
- output_weight_gradient: float32 [768, 768], P('tp')
- output_bias_gradient: float32 [768], replicated
- second_gain_gradient: float32 [768], replicated
- second_bias_gradient: float32 [768], replicated
- inner_weight_gradient: float32 [768, 3072], P(None, 'tp')
- inner_bias_gradient: float32 [3072], P('tp')
- outer_weight_gradient: float32 [3072, 768], P('tp')
- outer_bias_gradient: float32 [768], replicated
Inputs may be any that keep to these rules, and one draw needn't show every extreme that they name: `block_owner`: all blocks of one sequence carry one number, and pieces of a data group share the same blocks. A sequence covers 8192 // 256 or twice that many consecutive blocks of every piece, so it has 8192 or 16384 tokens; its number is the index of its last 8192-token unit, so numbers rise along a row, differ between sequences, and the last block of every row carries 1 - 1.
All inputs are finite; a program needn't handle non-finite values.
Results may differ from a plain program's by a relative error of at most 0.015.
Values may be sent and summed in bfloat16 or wider, within the bound.
A program may use at most 128 MiB of HBM per device.

v0:
```python
import functools
from types import SimpleNamespace

import jax
import jax.numpy as jnp
from jax import lax
from jax.experimental import pallas as pl
from jax.experimental.pallas import tpu as pltpu
from jax.sharding import PartitionSpec as P

MESH = pl.DeviceIdType.MESH

HD = 64
BLOCK = 64
CHUNK = 256
EPSILON = 1e-05
F32 = jnp.float32
BF16 = jnp.bfloat16
ALL = ("dp", "ctx", "tp")


def ein(spec, a, b):
    return jnp.einsum(spec, a, b, preferred_element_type=F32)


def layer_norm(v, gain, offset):
    c = v - jnp.mean(v, axis=-1, keepdims=True)
    r = lax.rsqrt(jnp.mean(c * c, axis=-1, keepdims=True) + EPSILON)
    n = c * r
    return n * gain + offset, n, r


def layer_norm_back(e, n, r, gain):
    m = e * gain
    back = r * (
        m - jnp.mean(m, axis=-1, keepdims=True) - n * jnp.mean(m * n, axis=-1, keepdims=True)
    )
    return back, jnp.sum(e * n, axis=0), jnp.sum(e, axis=0)


def gelu_parts(s):
    t = jnp.tanh(0.7978845608028654 * (s + 0.044715 * s * s * s))
    slope = 0.7978845608028654 * (1.0 + 3.0 * 0.044715 * s * s)
    return 0.5 * s * (1.0 + t), 0.5 * (1.0 + t) + 0.5 * s * (1.0 - t * t) * slope


def feature_map(q, weight, offset):
    u = ein("thd,hde->the", q, weight) + offset
    up, down = jax.nn.softmax(u, axis=-1), jax.nn.softmax(-u, axis=-1)
    return up, down, jnp.concatenate([up, down], axis=-1).astype(BF16)


def feature_back(delta, up, down, q, weight):
    d, dd = delta[..., :HD], delta[..., HD:]
    du = up * (d - jnp.sum(up * d, axis=-1, keepdims=True)) - down * (
        dd - jnp.sum(down * dd, axis=-1, keepdims=True)
    )
    low = du.astype(BF16)
    return ein("the,hde->thd", low, weight), ein("thd,the->hde", q, low), jnp.sum(du, axis=0)


HD = 64
BLOCK = 64
CHUNK = 256
EPSILON = 1e-05
F32 = jnp.float32
BF16 = jnp.bfloat16
ALL = ("dp", "ctx", "tp")


def ein(spec, a, b):
    return jnp.einsum(spec, a, b, preferred_element_type=F32)


def layer_norm(v, gain, offset):
    c = v - jnp.mean(v, axis=-1, keepdims=True)
    r = lax.rsqrt(jnp.mean(c * c, axis=-1, keepdims=True) + EPSILON)
    n = c * r
    return n * gain + offset, n, r


def layer_norm_back(e, n, r, gain):
    m = e * gain
    back = r * (
        m - jnp.mean(m, axis=-1, keepdims=True) - n * jnp.mean(m * n, axis=-1, keepdims=True)
    )
    return back, jnp.sum(e * n, axis=0), jnp.sum(e, axis=0)


def gelu_parts(s):
    t = jnp.tanh(0.7978845608028654 * (s + 0.044715 * s * s * s))
    slope = 0.7978845608028654 * (1.0 + 3.0 * 0.044715 * s * s)
    return 0.5 * s * (1.0 + t), 0.5 * (1.0 + t) + 0.5 * s * (1.0 - t * t) * slope


def feature_map(q, weight, offset):
    u = ein("thd,hde->the", q, weight) + offset
    up, down = jax.nn.softmax(u, axis=-1), jax.nn.softmax(-u, axis=-1)
    return up, down, jnp.concatenate([up, down], axis=-1).astype(BF16)


def feature_back(delta, up, down, q, weight):
    d, dd = delta[..., :HD], delta[..., HD:]
    du = up * (d - jnp.sum(up * d, axis=-1, keepdims=True)) - down * (
        dd - jnp.sum(down * dd, axis=-1, keepdims=True)
    )
    low = du.astype(BF16)
    return ein("the,hde->thd", low, weight), ein("thd,the->hde", q, low), jnp.sum(du, axis=0)


def place():
    d, c, t = lax.axis_index("dp"), lax.axis_index("ctx"), lax.axis_index("tp")
    y, core = c // 2, lax.rem(c, 2)
    return SimpleNamespace(d=d, c=c, t=t, y=y, core=core, q=d * 2 + y,
        x_nb=(1 - d, c, t), y_nb=(d, (1 - y) * 2 + core, t), core_nb=(d, y * 2 + 1 - core, t),
        qx=(1 - d) * 2 + y, qy=d * 2 + 1 - y, qd=(1 - d) * 2 + 1 - y)

def plane_peer(p, r):
    d = 1 - p.d if r & 4 else p.d
    y = 1 - p.y if r & 2 else p.y
    core = 1 - p.core if r & 1 else p.core
    return (d, y * 2 + core, p.t), d * 4 + y * 2 + core


def greet(p):
    bar = pltpu.get_barrier_semaphore()
    peers = [plane_peer(p, r)[0] for r in range(1, 8)]
    peers += [(p.d, p.c, lax.rem(p.t + k, 4)) for k in (1, 2, 3)]
    for peer in peers:
        pl.semaphore_signal(bar, inc=1, device_id=peer, device_id_type=MESH)


def met(p):
    pl.semaphore_wait(pltpu.get_barrier_semaphore(), 10)


def nearest(t):
    return [
        jnp.where(t < 2, 1, 3),
        jnp.where(t == 0, 2, jnp.where(t == 1, 3, jnp.where(t == 2, 1, 2))),
        jnp.where(t == 0, 3, jnp.where(t == 3, 1, 2)),
    ]


class Gather:
    def __init__(self, p, buf, sems, send, index):
        self.p, self.buf, self.sems, self.send, self.i = p, buf, sems, send.at[index], index
        self.rows = buf.shape[1]
        self.piece = self.rows // 8
        self.half = self.piece // 2
    def at(self, t, q, core, half=None):
        start = q * (2 * self.piece) + core * self.piece
        size = self.piece
        if half is not None:
            start, size = start + half * self.half, self.half
        return self.buf.at[t, pl.ds(pl.multiple_of(start, 16), size)]
    def shard(self, k): return lax.rem(self.p.t + k, 4)
    def copy(self, ref, kind, k, peer):
        n = 0 if kind == "z" else 2 if kind == "c" else 1
        recv = self.sems[kind].at[self.i, k - 1]
        return pltpu.make_async_remote_copy(
            ref, ref, self.send.at[n], recv, device_id=peer, device_id_type=MESH
        )

    def go(self, *a):
        self.copy(*a).start()

    def first(self):
        p = self.p
        ref = self.at(p.t, p.q, p.core)
        for k in (1, 2, 3):
            self.go(ref, "z", 4 - k, (p.d, p.c, lax.rem(p.t + k, 4)))

    def first_hop(self):
        p = self.p
        ref = self.at(p.t, p.q, p.core)
        pl.when(p.t < 3)(lambda: self.go(ref, "z", 3, (p.d, p.c, p.t + 1)))
        pl.when(p.t > 0)(lambda: self.go(ref, "z", 1, (p.d, p.c, p.t - 1)))

    def zf(self, k):
        p, t = self.p, self.shard(k)
        ref = self.at(t, p.q, p.core)
        self.copy(ref, "z", k, p.x_nb).wait_recv()
        up = jnp.logical_and(t < p.t, p.t < 3)
        down = jnp.logical_and(t > p.t, p.t > 0)
        pl.when(up)(lambda: self.go(ref, "z", k - 1, (p.d, p.c, p.t + 1)))
        pl.when(down)(lambda: self.go(ref, "z", k + 1, (p.d, p.c, p.t - 1)))

    def spread(self, k):
        p = self.p
        ref = self.at(self.shard(k), p.q, p.core)
        self.go(ref, "x", k, p.x_nb)
        self.go(ref, "y", k, p.y_nb)

    def z(self, k):
        p, t = self.p, self.shard(k)
        ref = self.at(t, p.q, p.core)
        self.copy(ref, "z", k, p.x_nb).wait_recv()
        self.go(ref, "x", k, p.x_nb); self.go(ref, "y", k, p.y_nb)
    def xy(self, k):
        p, t = self.p, self.shard(k)
        self.copy(self.at(t, p.qx, p.core), "x", k, p.x_nb).wait_recv()
        self.go(self.at(t, p.qx, p.core, 0), "fy", k, p.y_nb)
        self.copy(self.at(t, p.qy, p.core), "y", k, p.y_nb).wait_recv()
        self.go(self.at(t, p.qy, p.core, 1), "fx", k, p.x_nb)
    def diag(self, k):
        p, t = self.p, self.shard(k)
        self.copy(self.at(t, p.qd, p.core, 0), "fy", k, p.y_nb).wait_recv()
        self.copy(self.at(t, p.qd, p.core, 1), "fx", k, p.x_nb).wait_recv()
        for q in range(4):
            self.go(self.at(t, q, p.core), "c", k, p.core_nb)
    def done(self, k):
        p, t = self.p, self.shard(k)
        self.copy(self.buf.at[t, pl.ds(0, 4 * self.piece)], "c", k, p.core_nb).wait_recv()

    def drain(self, hops):
        p = self.p

        def wait(kind, ref):
            self.copy(ref, kind, 1, p.core_nb).wait_send()

        line = lambda n: wait("z", self.buf.at[0, pl.ds(0, n * self.piece)])
        if hops:
            ends = jnp.logical_or(p.t == 0, p.t == 3)
            pl.when(ends)(lambda: line(1))
            pl.when(jnp.logical_not(ends))(lambda: line(5))
        else:
            line(3)
        wait("x", self.buf.at[pl.ds(0, 3), pl.ds(0, 3 * self.piece)])
        wait("c", self.buf.at[pl.ds(0, 3), pl.ds(0, 4 * self.piece)])


def lanes(core):
    return pl.ds(pl.multiple_of(core * 384, 128), 384)


class Reduce:
    def __init__(self, p, i, G, X1, Y1, X2, Y2, Z, OUT, sems, send, own):
        self.p, self.i, self.G, self.OUT, self.sems = p, i, G, OUT, sems
        self.X1, self.Y1, self.X2, self.Y2, self.Z = X1, Y1, X2, Y2, Z
        self.half = G.shape[1]; self.qr = self.half // 4; self.hr = self.qr // 2
        self.send = send
        self.own = own
    def t(self, k): return lax.rem(self.p.t + k, 4)
    def rows(self, q, h): return pl.ds(pl.multiple_of(q * self.qr + h * self.hr, 16), self.hr)
    def rdma(self, src, dst, kind, k, peer):
        n = 1 if kind == "z" else 0 if kind != "f" else 3 if k == 4 else 2
        return pltpu.make_async_remote_copy(
            src,
            dst,
            self.send.at[self.i, n],
            self.sems[kind].at[self.i, k],
            device_id=peer,
            device_id_type=MESH,
        )

    def go(self, *a):
        self.rdma(*a).start()

    def got(self, ref, kind, k):
        self.rdma(ref, ref, kind, k, self.p.x_nb).wait_recv()
    def one(self, k):
        p, t = self.p, self.t(k)
        for j in range(2):
            self.go(self.G.at[t, self.rows((1 - p.d) * 2 + j, 0)], self.X1.at[k, j], "x1", k, p.x_nb)
            self.go(self.G.at[t, self.rows(j * 2 + 1 - p.y, 1)], self.Y1.at[k, j], "y1", k, p.y_nb)
    def two(self, k):
        p, t, G = self.p, self.t(k), self.G
        self.got(self.X1.at[k], "x1", k)
        for j in range(2):
            r = self.rows(p.d * 2 + j, 0)
            G[t, r] = G[t, r] + self.X1[k, j]
        self.go(G.at[t, self.rows(p.qy, 0)], self.Y2.at[k], "y2", k, p.y_nb)
        self.got(self.Y1.at[k], "y1", k)
        for j in range(2):
            r = self.rows(j * 2 + p.y, 1)
            G[t, r] = G[t, r] + self.Y1[k, j]
        self.go(G.at[t, self.rows(p.qx, 1)], self.X2.at[k], "x2", k, p.x_nb)
    def three(self, k):
        p, t, G = self.p, self.t(k), self.G
        for h, (kind, R) in enumerate((("y2", self.Y2), ("x2", self.X2))):
            self.got(R.at[k], kind, k)
            r = self.rows(p.q, h)
            G[t, r] = G[t, r] + R[k]
        if not isinstance(k, int):
            whole = pl.ds(pl.multiple_of(p.q * self.qr, 16), self.qr)
            self.go(G.at[t, whole], self.Z.at[3 - k], "z", 3 - k, (p.d, p.c, t))
    def piece(self, q, core, h=None):
        start, size = q * self.qr, self.qr
        if h is not None:
            start, size = start + h * self.hr, self.hr
        return self.OUT.at[pl.ds(pl.multiple_of(start, 16), size), lanes(core)]

    def final(self):
        p = self.p
        whole = pl.ds(pl.multiple_of(p.q * self.qr, 16), self.qr)
        total = self.G[p.t, whole].astype(F32)
        for k in range(3):
            self.got(self.Z.at[k], "z", k)
            total = total + self.Z[k].astype(F32)
        ref = self.piece(p.q, p.core)
        mine = self.G.at[p.t, whole]
        mine[...] = total.astype(BF16)
        self.go(mine, ref, "f", 0, p.x_nb)
        self.go(mine, ref, "f", 1, p.y_nb)
        self.own_copy().start()

    def own_copy(self):
        p = self.p
        whole = pl.ds(pl.multiple_of(p.q * self.qr, 16), self.qr)
        return pltpu.make_async_copy(
            self.G.at[p.t, whole], self.piece(p.q, p.core), self.own.at[self.i]
        )

    def spread(self):
        p = self.p
        ref = self.piece(p.qx, p.core); self.got(ref, "f", 0)
        ref = self.piece(p.qx, p.core, 0); self.go(ref, ref, "f", 2, p.y_nb)
        ref = self.piece(p.qy, p.core); self.got(ref, "f", 1)
        ref = self.piece(p.qy, p.core, 1); self.go(ref, ref, "f", 3, p.x_nb)
    def corner(self):
        p = self.p
        self.own_copy().wait()
        self.got(self.piece(p.qd, p.core, 0), "f", 2); self.got(self.piece(p.qd, p.core, 1), "f", 3)
        ref = self.OUT.at[:, lanes(p.core)]
        self.go(ref, ref, "f", 4, p.core_nb)
    def end(self):
        p = self.p
        self.got(self.OUT.at[:, lanes(1 - p.core)], "f", 4)
        rows = 3 * self.half // 4
        sizes = (
            ("x1", 0, self.G.at[pl.ds(0, 3)]),
            ("z", 0, self.Z),
            ("f", 0, self.G.at[0, pl.ds(0, rows)]),
            ("f", 4, self.G.at[0]),
        )
        for kind, k, ref in sizes:
            self.rdma(ref, ref, kind, k, p.core_nb).wait_send()


GATHER_SEMS = ("z", "x", "y", "fx", "fy", "c")
SEMS = ("x1", "y1", "x2", "y2", "z", "f")


def dot(a, b, ca, cb):
    return lax.dot_general(a, b, (((ca,), (cb,)), ((), ())), preferred_element_type=F32)


def loop(n, step):
    def body(i, carry):
        step(i)
        return carry

    lax.fori_loop(0, n, body, 0)


def ds(i, n):
    return pl.ds(pl.multiple_of(i * n, n), n)


class Scan:
    def __init__(self, p, later, total, up, down, got, sems):
        self.p, self.later, self.total, self.up_ref, self.down_ref = p, later, total, up, down
        self.from_core, self.from_y, self.from_below, self.from_above = [got.at[i] for i in range(4)]
        self.sems = sems

    def rdma(self, src, dst, g, i, peer):
        h, i = self.heads(g), 4 * i + g
        return pltpu.make_async_remote_copy(
            src.at[h], dst.at[h], self.sems.at[0, i], self.sems.at[1, i], device_id=peer, device_id_type=MESH
        )

    def core_copy(self, g):
        return self.rdma(self.total, self.from_core, g, 0, self.p.core_nb)

    def y_copy(self, g):
        return self.rdma(self.up_ref, self.from_y, g, 1, self.p.y_nb)

    def line_copy(self, g, upward):
        p = self.p
        if upward:
            return self.rdma(self.up_ref, self.from_below, g, 2, (p.d, p.c, p.t + 1))
        return self.rdma(self.down_ref, self.from_above, g, 3, (p.d, p.c, p.t - 1))

    def heads(self, g):
        return pl.ds(3 * g, 3)

    def begin(self, g):
        h = self.heads(g)
        zero = jnp.zeros((3, 80, 128), BF16)

        @pl.when(self.p.t == 0)
        def _():
            self.from_below[h] = zero

        @pl.when(self.p.t == 3)
        def _():
            self.from_above[h] = zero

        self.core_copy(g).start()

    def pair(self, g):
        h = self.heads(g)
        self.core_copy(g).wait_recv()
        self.up_ref[h] = self.total[h] + self.from_core[h]
        self.y_copy(g).start()

    def column(self, g):
        p, h = self.p, self.heads(g)
        core, y = p.core.astype(F32), p.y.astype(F32)
        if self.later:
            core, y = 1.0 - core, 1.0 - y
        return core * self.from_core[h].astype(F32) + y * self.from_y[h].astype(F32)

    def hop(self, g, upward):
        h, t = self.heads(g), self.p.t
        has, sends = (t > 0, t < 3) if upward else (t < 3, t > 0)
        c = self.line_copy(g, upward)
        got = self.from_below if upward else self.from_above
        out = self.up_ref if upward else self.down_ref

        @pl.when(has)
        def _():
            c.wait_recv()

        @pl.when(sends)
        def _():
            value = self.column(g) + got[h].astype(F32)
            if upward != self.later:
                value = value + self.total[h].astype(F32)
            out[h] = value.astype(BF16)
            c.start()

    def chain(self, g):
        c = self.y_copy(g)
        c.wait_recv()
        c.wait_send()
        pl.when(self.p.t < 2)(lambda: self.hop(g, True))
        pl.when(self.p.t >= 2)(lambda: self.hop(g, False))

    def relay(self, g):
        pl.when(self.p.t == 1)(lambda: self.hop(g, False))
        pl.when(self.p.t == 2)(lambda: self.hop(g, True))

    def last(self, g):
        pl.when(self.p.t == 0)(lambda: self.hop(g, False))
        pl.when(self.p.t == 3)(lambda: self.hop(g, True))

    def sum(self, g):
        h = self.heads(g)
        return self.column(g) + self.from_below[h].astype(F32) + self.from_above[h].astype(F32)

    def drain(self):
        for g in range(4):
            self.core_copy(g).wait_send()
            pl.when(self.p.t < 3)(lambda g=g: self.line_copy(g, True).wait_send())
            pl.when(self.p.t > 0)(lambda g=g: self.line_copy(g, False).wait_send())


class Small:
    def __init__(self, p, low, full, plane, line, mid, out, sems, send, own):
        self.p, self.low, self.full, self.plane, self.line, self.mid, self.out = (
            p, low, full, plane, line, mid, out
        )
        self.sems, self.send, self.own = sems, send, own
        self.me = p.d * 4 + p.c

    def rdma(self, src, dst, i, peer):
        n = 0 if i < 7 else 1 if i < 10 else 2
        return pltpu.make_async_remote_copy(
            src, dst, self.send.at[n], self.sems.at[i], device_id=peer, device_id_type=MESH
        )

    def go(self, *a):
        self.rdma(*a).start()

    def begin(self):
        for r in range(1, 8):
            peer, j = plane_peer(self.p, r)
            self.go(self.low.at[ds(j, 32)], self.plane.at[r - 1], r - 1, peer)

    def across(self):
        p = self.p
        for r in range(1, 8):
            self.rdma(self.plane.at[r - 1], self.plane.at[r - 1], r - 1, p.x_nb).wait_recv()
        for t in range(4):
            total = self.full[t, ds(self.me, 32)]
            for r in range(7):
                total = total + self.plane[r, :, 128 * t : 128 * t + 128].astype(F32)
            self.full[t, ds(self.me, 32)] = total
            self.mid[t] = total.astype(BF16)
        for k in (1, 2, 3):
            t = lax.rem(p.t + k, 4)
            self.go(self.mid.at[t], self.line.at[3 - k], 10 - k, (p.d, p.c, t))

    def final(self):
        p = self.p
        total = self.full[p.t, ds(self.me, 32)]
        for k in range(3):
            self.rdma(self.line.at[k], self.line.at[k], 7 + k, p.x_nb).wait_recv()
            total = total + self.line[k].astype(F32)
        self.mid[4] = total.astype(BF16)
        ref = self.out.at[ds(self.me, 32)]
        for r in range(1, 8):
            self.go(self.mid.at[4], ref, 9 + r, plane_peer(p, r)[0])
        pltpu.make_async_copy(self.mid.at[4], ref, self.own).start()

    def end(self):
        pltpu.make_async_copy(self.mid.at[4], self.out.at[ds(self.me, 32)], self.own).wait()
        for r in range(1, 8):
            peer, j = plane_peer(self.p, r)
            ref = self.out.at[ds(j, 32)]
            self.rdma(ref, ref, 9 + r, peer).wait_recv()
        for i, ref in ((0, self.plane), (7, self.line), (10, self.plane.at[:, :, pl.ds(0, 128)])):
            self.rdma(ref, ref, i, self.p.core_nb).wait_send()


def layer_rows(v):
    c = v - jnp.mean(v, axis=-1, keepdims=True)
    r = lax.rsqrt(jnp.mean(c * c, axis=-1, keepdims=True) + EPSILON)
    return c * r, r


def fold(v):
    total = v[:8]
    for i in range(1, v.shape[0] // 8):
        total = total + v[8 * i : 8 * i + 8]
    return total


def layer_back(e, n, r, gain):
    m = e * gain
    return r * (
        m - jnp.mean(m, axis=-1, keepdims=True) - n * jnp.mean(m * n, axis=-1, keepdims=True)
    )


def block_kernel(m):
    p = place()
    t0 = p.t
    X, CT, S, WA, W1, W2 = m.X, m.CT, m.S, m.WA, m.W1, m.W2
    VEC, H1, H2, X2, ACC_O, ACC_E = m.VEC, m.H1, m.H2, m.X2, m.ACC_O, m.ACC_E
    MIX, PH, VX, AT, PX, SL, OT, RD = m.MIX, m.PH, m.VX, m.AT, m.PX, m.SL, m.OT, m.RD
    A, DF, GS, FW, BC, IB, SUMS = m.A, m.DF, m.GS, m.FW, m.BC, m.IB, m.SUMS
    ld = m.ld
    greet(p)
    loads = [
        pltpu.make_async_copy(m.wm, WA.at[t0, pl.ds(0, 576)], ld.at[0]),
        pltpu.make_async_copy(m.wo, WA.at[t0, pl.ds(576, 192)], ld.at[1]),
        pltpu.make_async_copy(m.x, X, ld.at[2]),
        pltpu.make_async_copy(m.w1, W1.at[t0], ld.at[3]),
        pltpu.make_async_copy(m.w2, W2.at[t0], ld.at[4]),
        pltpu.make_async_copy(m.g, CT, ld.at[5]),
    ]
    raw = [(m.fw, m.FWI), (m.mb, m.MBI), (m.fb, m.FBI)]
    raw += [(ref, m.VECI.at[i, pl.ds(0, 6)]) for i, ref in enumerate(m.vectors)]
    raw = [pltpu.make_async_copy(src, dst, ld.at[8 + i]) for i, (src, dst) in enumerate(raw)]
    for c in raw + loads:
        c.start()
    for c in raw:
        c.wait()

    for h in range(3):
        pair = [m.FWI[i, h].astype(F32) for i in range(2)]
        S[t0, 64 * h : 64 * h + 64] = jnp.concatenate(pair, axis=1).astype(BF16)
    zero = jnp.zeros((1, HD), F32)
    rows = []
    for j in range(3):
        row = m.MBI[j : j + 1].astype(F32)
        rows += [
            jnp.concatenate([row[:, HD * h : HD * h + HD], zero], axis=1) for h in range(3)
        ]
    for h in range(3):
        row = m.FBI[h].astype(F32)
        rows.append(jnp.concatenate([row[0:1], row[1:2]], axis=1))
    rows.append(jnp.zeros((4, 128), F32))
    S[t0, 192:208] = jnp.concatenate(rows, axis=0).astype(BF16)
    rows = [m.VECI[6].astype(F32)[0:6], jnp.zeros((42, 128), F32)]
    S[t0, 208:256] = jnp.concatenate(rows, axis=0).astype(BF16)
    for k in range(6):
        value = m.VECI[k].astype(F32)
        for i in range(6):
            VEC[k : k + 1, 128 * i : 128 * i + 128] = value[i : i + 1]

    gs, gw, g1, g2 = gathers = [
        Gather(p, b, m.gather_sems, m.gather_send, i) for i, b in enumerate((S, WA, W1, W2))
    ]
    K = nearest(t0)
    shard = gs.shard
    loads[0].wait()
    loads[1].wait()
    met(p)
    gw.first()
    gs.first()

    loads[2].wait()

    def norm1(i):
        r = ds(i, 128)
        n, _ = layer_rows(X[r].astype(F32))
        H1[r] = (n * VEC[0:1] + VEC[1:2]).astype(BF16)

    loop(4, norm1)
    ones_row = jnp.where(lax.broadcasted_iota(jnp.int32, (16, 512), 0) == 0, 1.0, 0.0).astype(BF16)

    def init(h):
        VX[h, 64:80] = ones_row

    loop(12, init)
    SUMS[...] = jnp.zeros_like(SUMS)

    def small(t):
        BC[...] = S[t, 192:208].astype(F32).T
        rows = S[t, 208:224].astype(F32)
        for i in range(6):
            IB[t, :, 128 * i : 128 * i + 128] = rows[i : i + 1]
        for h in range(3):
            w = S[t, 64 * h : 64 * h + 64].astype(F32)
            FW[0, t * 3 + h] = w[:, :64].astype(BF16)
            FW[1, t * 3 + h] = w[:, 64:].astype(BF16)

    def mix(t):
        value = dot(WA[t, 0:576], H1[...], 1, 1)
        for j in range(3):
            for h in range(3):
                n = j * 3 + h
                part = (value[64 * n : 64 * n + 64] + BC[0:64, n : n + 1]).astype(BF16)
                if j < 2:
                    MIX[t, 64 * n : 64 * n + 64] = part
                else:
                    VX[t * 3 + h, 0:64] = part

    def features(t):
        for h in range(3):
            for i in range(2):
                u = dot(FW[i, t * 3 + h], MIX[t, 192 * i + 64 * h : 192 * i + 64 * h + 64], 0, 0)
                u = u + BC[64 * i : 64 * i + 64, 9 + h : 10 + h]
                e = jnp.exp(u - jnp.max(u, axis=0, keepdims=True))
                PH[i, t * 3 + h, 0:64] = (e / jnp.sum(e, axis=0, keepdims=True)).astype(BF16)
                e = jnp.exp(jnp.min(u, axis=0, keepdims=True) - u)
                PH[i, t * 3 + h, 64:128] = (e / jnp.sum(e, axis=0, keepdims=True)).astype(BF16)

    def states(t):
        def one(i):
            h = t * 3 + i
            s0 = dot(VX[h, :, 0:256], PH[1, h, :, 0:256], 1, 1)
            s1 = dot(VX[h, :, 256:512], PH[1, h, :, 256:512], 1, 1)
            SL[h] = s0
            m.TOT[h] = (s0 + s1).astype(BF16)

        loop(3, one)

    small(t0)
    mix(t0)
    features(t0)
    states(t0)
    both = (g1, g2)
    for n, k in enumerate(K):
        gw.z(k)
        gs.z(k)
        if n == 1:
            loads[3].wait()
            loads[4].wait()
            for g in both:
                g.first_hop()
    for k in K:
        gw.xy(k)
        gs.xy(k)
    for k in K:
        gw.diag(k)
        gs.diag(k)
    middle = jnp.logical_or(t0 == 1, t0 == 2)
    for g in both:
        g.zf(K[0])
        g.spread(K[0])
    for g in both:
        pl.when(middle)(lambda g=g: g.zf(K[1]))
    def arrived(n):
        k = jnp.where(n == 0, K[0], jnp.where(n == 1, K[1], K[2]))
        gs.done(k)
        gw.done(k)
        t = shard(k)
        small(t)
        mix(t)
        features(t)
        states(t)

    loop(3, arrived)
    scan = Scan(p, False, m.TOT, m.UP, m.DOWN, m.got_f, m.scan_f)
    for g in range(4):
        scan.begin(g)
    causal = lax.broadcasted_iota(jnp.int32, (256, 256), 0) <= lax.broadcasted_iota(
        jnp.int32, (256, 256), 1
    )

    def scores(h):
        for j in range(2):
            c = slice(256 * j, 256 * j + 256)
            a = dot(PH[1, h, :, c], PH[0, h, :, c], 0, 0)
            AT[h, j] = jnp.where(causal, a, 0.0).astype(BF16)

    for g in both:
        g.zf(jnp.where(middle, K[2], K[1]))
    for g in range(4):
        scan.pair(g)
    loop(12, scores)
    for g in range(4):
        scan.chain(g)
    for g in both:
        g.xy(K[0])
        g.spread(K[1])
    for g in both:
        pl.when(jnp.logical_not(middle))(lambda g=g: g.zf(K[2]))
    for g in range(4):
        scan.relay(g)
    for g in both:
        g.spread(K[2])

    def enter(first):
        for g in range(4):
            scan.last(g)
            value = scan.sum(g)
            h = scan.heads(g)
            PX[h, first] = value.astype(BF16)
            PX[h, 1 - first] = (value + SL[h]).astype(BF16)

    enter(0)

    def attend(h):
        for j in range(2):
            c = slice(256 * j, 256 * j + 256)
            num = dot(PX[h, j], PH[0, h, :, c], 1, 0) + dot(VX[h, :, c], AT[h, j], 1, 0)
            r = 1.0 / num[64:65]
            RD[h, :, c] = r
            OT[ds(h, 64), c] = (num[0:64] * r).astype(BF16)

    loop(12, attend)

    def norm2(i):
        r = ds(i, 256)
        total = X[r].astype(F32) + VEC[2:3]
        for t in range(4):
            total = total + dot(OT[192 * t : 192 * t + 192, r], WA[t, 576:768], 0, 0)
        X2[r] = total
        n, _ = layer_rows(total)
        H2[r] = (n * VEC[3:4] + VEC[4:5]).astype(BF16)
        ACC_O[r] = total + VEC[5:6]
        ACC_E[r] = jnp.zeros((256, 768), F32)

    loop(2, norm2)

    R = [
        Reduce(p, i, m.G[i], *m.land[i][1:], m.Z[i], m.outs[i], m.reduce_sems, m.reduce_send, m.own)
        for i in range(4)
    ]
    core_sems, STAGE = m.r_core, m.STAGE
    outgoing = []

    def core_copy(src, i, k):
        ref = m.land[i][0].at[shard(k)]
        return pltpu.make_async_remote_copy(
            ref if src is None else src,
            ref,
            core_sems.at[0, i, k],
            core_sems.at[1, i, k],
            device_id=p.core_nb,
            device_id_type=MESH,
        )

    def hand(i, k, value):
        slot = len(outgoing) % 2
        if len(outgoing) >= 2:
            outgoing[-2].wait_send()
        ref = STAGE.at[slot, pl.ds(0, R[i].half)]
        ref[...] = value(1 - p.core).astype(BF16)
        c = core_copy(ref, i, k)
        c.start()
        outgoing.append(c)
        R[i].G[shard(k)] = value(p.core).astype(BF16)

    def meet(i, k):
        t = shard(k)
        G, C = R[i].G, m.land[i][0]
        core_copy(None, i, k).wait_recv()

        def add(j):
            r = ds(j, 96)
            G[t, r] = G[t, r] + C[t, r]

        loop(R[i].half // 96, add)
        R[i].one(k)

    def hidden(t, slot):
        def rows(i):
            r = ds(i, 256)
            f = dot(H2[r], W1[t], 1, 0) + IB[t]
            th = jnp.tanh(0.7978845608028654 * (f + 0.044715 * f * f * f))
            a = (0.5 * f * (1.0 + th)).astype(BF16)
            A[slot, r] = a
            slope = 0.5 * (1.0 + th) + 0.5 * f * (1.0 - th * th) * (
                0.7978845608028654 * (1.0 + 3.0 * 0.044715 * f * f)
            )
            df = (dot(CT[r], W2[t], 1, 1) * slope).astype(BF16)
            DF[slot, r] = df
            m.DIB[t] += fold(df.astype(F32))
            ACC_O[r] += dot(a, W2[t], 1, 0)
            ACC_E[r] += dot(df, W1[t], 1, 1)

        loop(2, rows)

    def hand_hidden(k, slot):
        hand(0, k, lambda core: dot(A[slot], CT[:, lanes(core)], 0, 0))
        hand(1, k, lambda core: dot(H2[...], DF[slot, :, lanes(core)], 0, 0))

    m.DIB[...] = jnp.zeros_like(m.DIB)
    order = [0] + K
    loads[5].wait()
    for g in both:
        g.diag(K[0])
        g.xy(K[1])
    hidden(t0, 0)
    for g in both:
        g.xy(K[2])
        g.diag(K[1])
    hand_hidden(0, 0)
    for n, k in enumerate(K):
        g1.done(k)
        g2.done(k)
        hidden(shard(k), n // 2)
        if n == 0:
            for g in both:
                g.diag(K[2])
        if n < 2:
            for i in range(2):
                meet(i, order[n])
        if n < 1:
            hand_hidden(k, 0)
    for g in both:
        g.drain(True)
    RES, GG = W1.at[2, pl.ds(0, 512)], W1.at[3, pl.ds(0, 512)]

    def dne(h):
        start = pl.multiple_of(lax.rem(h, 9) * 80, 16)
        return W2.at[h // 9, pl.ds(start, 80), pl.ds(0, 512)]

    def du_of(h):
        return W1.at[h // 6, ds(lax.rem(h, 6), 128), pl.ds(0, 512)]

    def dv_of(h):
        return W2.at[2, ds(h, 64), pl.ds(0, 512)]

    def back2(i):
        r = ds(i, 128)
        n, s = layer_rows(X2[r])
        e = ACC_E[r]
        g = CT[r].astype(F32)
        dx = g + layer_back(e, n, s, VEC[3:4])
        SUMS[3] += fold(e * n)
        SUMS[4] += fold(e)
        SUMS[2] += fold(dx)
        SUMS[5] += fold(g)
        X2[r] = dx
        GG[r] = dx.astype(BF16)

    loop(4, back2)
    DX = X2
    first_row = lax.broadcasted_iota(jnp.int32, (16, 512), 0) == 0

    scan.drain()
    scan = Scan(p, True, m.TOT, m.UP, m.DOWN, m.got_b, m.scan_b)

    def states_back(t):
        value = dot(WA[t, 576:768], GG[...], 1, 1).astype(BF16).astype(F32)
        for i in range(3):
            h = 3 * t + i
            do = value[64 * i : 64 * i + 64]
            r = RD[h]
            o = OT[ds(h, 64)].astype(F32)
            ref = dne(h)
            ref[0:64] = (do * r).astype(BF16)
            dden = -jnp.sum(do * o, axis=0, keepdims=True) * r
            ref[64:80] = jnp.where(first_row, dden, 0.0).astype(BF16)
            s0 = dot(ref[:, 0:256], PH[0, h, :, 0:256], 1, 1)
            s1 = dot(ref[:, 256:512], PH[0, h, :, 256:512], 1, 1)
            SL[h] = s1
            m.TOT[h] = (s0 + s1).astype(BF16)

    def give(t):
        states_back(t)
        scan.begin(t)

    loop(4, give)
    hand(0, order[2], lambda core: dot(A[0], CT[:, lanes(core)], 0, 0))
    for g in range(4):
        scan.pair(g)
    for i in range(2):
        R[i].two(order[0])
    hand(1, order[2], lambda core: dot(H2[...], DF[0, :, lanes(core)], 0, 0))
    for i in range(2):
        R[i].two(order[1])

    def feature_back(i, h, delta):
        delta = delta.astype(BF16).astype(F32)
        up, down = PH[i, h, 0:64].astype(F32), PH[i, h, 64:128].astype(F32)
        d, dd = delta[0:64], delta[64:128]
        du = up * (d - jnp.sum(up * d, axis=0, keepdims=True)) - down * (
            dd - jnp.sum(down * dd, axis=0, keepdims=True)
        )
        du_of(h)[64 * i : 64 * i + 64] = du.astype(BF16)

    def query_back(h):
        parts = []
        ref, dv = dne(h), dv_of(h)
        for j in range(2):
            c = slice(256 * j, 256 * j + 256)
            value = ref[:, c]
            dv[:, c] = dot(ref[0:64, c], AT[h, j], 1, 1).astype(BF16)
            da = dot(VX[h, :, c], value, 0, 0)
            da = jnp.where(causal, da, 0.0).astype(BF16)
            AT[h, j] = da
            parts.append(dot(PH[1, h, :, c], da, 1, 0) + dot(PX[h, j], value, 0, 0))
        feature_back(0, h, jnp.concatenate(parts, axis=1))

    ones8 = jnp.ones((8, 512), BF16)
    left = lax.broadcasted_iota(jnp.int32, (64, 128), 1) < 64
    GS[:, 192:256] = jnp.zeros((4, 64, 128), F32)

    def bias_row(t, j, i):
        ref = MIX[t, ds(3 * j + i, 64)]
        GS[t, pl.ds(192 + 3 * j + i, 1), 0:64] = dot(ones8, ref, 1, 1)[0:1]

    def early(k):
        t = shard(k)
        def one(i):
            h = t * 3 + i
            rows = ds(i, 64)
            du = du_of(h)[0:64]
            GS[t, rows, 0:64] = dot(MIX[t, rows], du, 1, 1)
            MIX[t, rows] = dot(FW[0, h], du, 1, 0).astype(BF16)
            bias_row(t, 0, i)

        loop(3, one)

        def value(core):
            both = [
                dot(MIX[t, 0:192], H1[:, lanes(core)], 1, 0),
                dot(OT[ds(t, 192)], GG[:, lanes(core)], 1, 0),
            ]
            return jnp.concatenate(both, axis=0)

        hand(2, k, value)

    def queries(g):
        loop(3, lambda i: query_back(3 * g + i))

    def ask(g):
        queries(g)
        scan.chain(g)

    loop(2, ask)
    for i in range(2):
        meet(i, order[2])
    loop(2, lambda g: ask(g + 2))
    for i in range(2):
        R[i].three(order[0])
        R[i].three(order[1])
    for g in range(4):
        scan.relay(g)
    hand_hidden(order[3], 1)
    RES[...] = ACC_O[...].astype(BF16)
    res_copy = pltpu.make_async_copy(RES, m.result, ld.at[6])
    res_copy.start()
    for i in range(2):
        R[i].two(order[2])
        meet(i, order[3])
    early(order[0])
    early(order[1])
    meet(2, order[0])
    R[0].three(order[2])
    early(order[2])
    meet(2, order[1])
    R[1].three(order[2])
    for i in range(2):
        R[i].two(order[3])
    early(order[3])
    meet(2, order[2])
    enter(1)

    def key_back(t, i):
        h = t * 3 + i
        parts, values = [], []
        for j in range(2):
            c = slice(256 * j, 256 * j + 256)
            q = PX[h, j]
            parts.append(dot(PH[0, h, :, c], AT[h, j], 1, 1) + dot(q, VX[h, :, c], 0, 0))
            values.append(dot(q[0:64], PH[1, h, :, c], 1, 0))
        feature_back(1, h, jnp.concatenate(parts, axis=1))
        dv = jnp.concatenate(values, axis=1) + dv_of(h)[...].astype(F32)
        MIX[t, ds(6 + i, 64)] = dv.astype(BF16)
        du = du_of(h)
        rows = ds(3 + i, 64)
        ref = ds(i, 64)
        GS[t, ref] = jnp.where(left, GS[t, ref], dot(MIX[t, rows], du[...], 1, 1))
        GS[t, pl.ds(201 + i, 1)] = dot(ones8, du[...], 1, 1)[0:1]
        MIX[t, rows] = dot(FW[1, h], du[64:128], 1, 0).astype(BF16)
        bias_row(t, 1, i)
        bias_row(t, 2, i)

    for n, k in enumerate(order):
        t = shard(k)
        loop(3, lambda i: key_back(t, i))
        hand(3, k, lambda core: dot(MIX[t, 192:576], H1[:, lanes(core)], 1, 0))
        if n == 0:
            meet(2, order[3])
            R[2].two(order[0])
            R[2].two(order[1])
        else:
            meet(3, order[n - 1])
        if n == 1:
            R[0].three(order[3])
            R[1].three(order[3])
            R[2].two(order[2])
        if n == 2:
            R[2].two(order[3])
            R[2].three(order[0])
            R[2].three(order[1])
            R[2].three(order[2])
            R[3].two(order[0])
        if n == 3:
            R[2].three(order[3])
            R[3].two(order[1])
            R[3].three(order[0])

    def back1(i):
        r = ds(i, 256)
        e = dot(MIX[0, :, r], WA[0, 0:576], 0, 0)
        for t in range(1, 4):
            e = e + dot(MIX[t, :, r], WA[t, 0:576], 0, 0)
        n, s = layer_rows(X[r].astype(F32))
        SUMS[0] += fold(e * n)
        SUMS[1] += fold(e)
        ACC_E[r] = DX[r] + layer_back(e, n, s, VEC[0:1])

    back1(0)
    meet(3, order[3])
    R[3].two(order[2])
    R[0].final()
    R[3].three(order[1])
    R[1].final()
    back1(1)
    R[0].spread()
    tok_copy = pltpu.make_async_copy(ACC_E, m.tokens_gradient, ld.at[7])
    tok_copy.start()
    for k in range(6):
        row = jnp.sum(SUMS[k], axis=0, keepdims=True)
        for i in range(6):
            for t in range(4):
                GS[t, 216 + 6 * k + i : 217 + 6 * k + i] = row[:, 128 * i : 128 * i + 128]
    for t in range(4):
        row = jnp.sum(m.DIB[t], axis=0, keepdims=True)
        for i in range(6):
            GS[t, 208 + i : 209 + i] = row[:, 128 * i : 128 * i + 128]
    GB = W2.at[3, pl.ds(0, 256), pl.ds(0, 512)]
    for t in range(4):
        GB[:, 128 * t : 128 * t + 128] = GS[t].astype(BF16)
    tiny = Small(p, GB, GS, m.plane, m.line, m.mid, m.outs[4], m.small_sems, m.small_send, m.own.at[4])
    tiny.begin()
    R[3].two(order[3])
    R[1].spread()
    R[3].three(order[2])
    R[2].final()
    R[0].corner()
    R[3].three(order[3])
    R[1].corner()
    tiny.across()
    R[2].spread()
    R[3].final()
    tiny.final()
    R[2].corner()
    R[3].spread()
    R[3].corner()
    for r in R:
        r.end()
    tiny.end()
    scan.drain()
    for c in outgoing[-2:]:
        c.wait_send()
    gs.drain(False)
    gw.drain(False)
    res_copy.wait()
    tok_copy.wait()


PACKS = ((768, 768), (768, 768), (384, 768), (384, 768))


def landing(rows):
    q, r = rows // 4, rows // 8
    shapes = ((4, rows), (4, 2, r), (4, 2, r), (4, r), (4, r))
    return [pltpu.VMEM((*shape, 384), BF16) for shape in shapes]


def block_call(*args):
    rows, width = args[0].shape
    flat = pltpu.VMEM((rows, width), BF16)
    wide = pltpu.VMEM((rows, width), F32)
    weights = pltpu.VMEM((4, 768, 768), BF16)
    state = pltpu.VMEM((12, 80, 128), BF16)
    dma = pltpu.SemaphoreType.DMA
    scratch = dict(
        X=flat,
        CT=flat,
        S=pltpu.VMEM((4, 256, 128), BF16),
        WA=weights,
        W1=weights,
        W2=weights,
        VEC=pltpu.VMEM((8, 768), F32),
        VECI=pltpu.VMEM((7, 8, 128), BF16),
        FWI=pltpu.VMEM((2, 3, HD, HD), BF16),
        MBI=pltpu.VMEM((3, 192), BF16),
        FBI=pltpu.VMEM((3, 2, HD), BF16),
        H1=flat,
        H2=flat,
        X2=wide,
        ACC_O=wide,
        ACC_E=wide,
        MIX=pltpu.VMEM((4, 576, rows), BF16),
        PH=pltpu.VMEM((2, 12, 128, rows), BF16),
        VX=pltpu.VMEM((12, 80, rows), BF16),
        AT=pltpu.VMEM((12, 2, 256, 256), BF16),
        PX=pltpu.VMEM((12, 2, 80, 128), BF16),
        SL=pltpu.VMEM((12, 80, 128), F32),
        OT=pltpu.VMEM((768, rows), BF16),
        RD=pltpu.VMEM((12, 1, rows), F32),
        A=pltpu.VMEM((2, rows, width), BF16),
        DF=pltpu.VMEM((2, rows, width), BF16),
        GS=pltpu.VMEM((4, 256, 128), F32),
        FW=pltpu.VMEM((2, 12, 64, 64), BF16),
        BC=pltpu.VMEM((128, 16), F32),
        IB=pltpu.VMEM((4, 1, 768), F32),
        SUMS=pltpu.VMEM((6, 8, 768), F32),
        DIB=pltpu.VMEM((4, 8, 768), F32),
        TOT=state,
        UP=state,
        DOWN=state,
        got_f=pltpu.VMEM((4, 12, 80, 128), BF16),
        got_b=pltpu.VMEM((4, 12, 80, 128), BF16),
        plane=pltpu.VMEM((7, 32, 512), BF16),
        line=pltpu.VMEM((3, 32, 128), BF16),
        mid=pltpu.VMEM((5, 32, 128), BF16),
        STAGE=pltpu.VMEM((2, 768, 384), BF16),
        G=[pltpu.VMEM((4, n, 384), BF16) for n, _ in PACKS],
        Z=[pltpu.VMEM((3, n // 4, 384), BF16) for n, _ in PACKS],
        land=[landing(n) for n, _ in PACKS],
        ld=dma((18,)),
        own=dma((5,)),
        r_core=dma((2, 4, 4)),
        gather_sems={k: dma((4, 3)) for k in GATHER_SEMS},
        gather_send=dma((4, 3)),
        reduce_sems={k: dma((4, n)) for k, n in zip(SEMS, (4, 4, 4, 4, 3, 5))},
        reduce_send=dma((4, 4)),
        small_sems=dma((17,)),
        small_send=dma((3,)),
        scan_f=dma((2, 16)),
        scan_b=dma((2, 16)),
    )
    leaves, tree = jax.tree.flatten(scratch, is_leaf=lambda v: not isinstance(v, (dict, list)))
    results = [
        jax.ShapeDtypeStruct((rows, width), BF16),
        jax.ShapeDtypeStruct((rows, width), F32),
        *[jax.ShapeDtypeStruct(pack, BF16) for pack in PACKS],
        jax.ShapeDtypeStruct((256, 128), BF16),
    ]

    def body(x, g, wm, wo, w1, w2, fw, mb, fb, *rest):
        vectors, (result, tokens_gradient), rest = rest[:7], rest[7:9], rest[9:]
        given = dict(
            x=x, g=g, wm=wm, wo=wo, w1=w1, w2=w2, fw=fw, mb=mb, fb=fb, vectors=vectors
        )
        block_kernel(
            SimpleNamespace(
                **given,
                result=result,
                tokens_gradient=tokens_gradient,
                outs=rest[:5],
                **jax.tree.unflatten(tree, rest[5:]),
            )
        )

    anywhere = pl.BlockSpec(memory_space=pl.ANY)
    return pl.pallas_call(
        body,
        out_shape=results,
        in_specs=[anywhere] * len(args),
        out_specs=[anywhere] * len(results),
        scratch_shapes=leaves,
        compiler_params=pltpu.CompilerParams(
            collective_id=0, has_side_effects=True, vmem_limit_bytes=67043328
        ),
        name="block",
    )(*args)


def finish_kernel(
    res, tok, outer, inner, q, o, k, v, small,
    res_o, tok_o, outer_o, inner_o, mixer_o, output_o, feature_o, mixer_bias_o, feature_bias_o, *vec_o,
):
    res_o[...] = res[...]
    tok_o[...] = tok[...]
    outer_o[...] = outer[...].astype(F32)
    inner_o[...] = inner[...].astype(F32)
    for i, ref in enumerate((q, k, v)):
        mixer_o[i] = ref[...].astype(F32)
    output_o[...] = o[...].astype(F32)

    @pl.when(pl.program_id(0) == 0)
    def _():
        rows = small[192:256].astype(F32)
        for h in range(3):
            w = small[64 * h : 64 * h + 64].astype(F32)
            feature_o[0, h] = w[:, :64]
            feature_o[1, h] = w[:, 64:]
            pair = rows[9 + h : 10 + h]
            feature_bias_o[h] = jnp.concatenate([pair[:, :64], pair[:, 64:]], axis=0)
            parts = [rows[3 * h + i : 3 * h + i + 1, :64] for i in range(3)]
            mixer_bias_o[h : h + 1] = jnp.concatenate(parts, axis=1)
        for i in range(6):
            vec_o[i][...] = rows[24 + 6 * i : 30 + 6 * i]
        vec_o[6][...] = rows[16:22]


def finish_call(res, tok, outer, inner, early, late, small):
    rows, width = res.shape
    steps = 4

    def spec(n, shift=0):
        return pl.BlockSpec((n, width), lambda i: (i + shift, 0))

    def whole(*shape):
        return pl.BlockSpec(shape, lambda i: (0,) * len(shape))

    def out(*shape):
        return jax.ShapeDtypeStruct(shape, F32)

    vectors = [(6, 128)] * 7
    return pl.pallas_call(
        finish_kernel,
        grid=(steps,),
        in_specs=[
            spec(rows // steps),
            spec(rows // steps),
            spec(768 // steps),
            spec(768 // steps),
            spec(192 // steps),
            spec(192 // steps, steps),
            spec(192 // steps),
            spec(192 // steps, steps),
            whole(256, 128),
        ],
        out_specs=[
            spec(rows // steps),
            spec(rows // steps),
            spec(768 // steps),
            spec(768 // steps),
            pl.BlockSpec((3, 192 // steps, width), lambda i: (0, i, 0)),
            spec(192 // steps),
            whole(2, 3, HD, HD),
            whole(3, 192),
            whole(3, 2, HD),
            *[whole(*v) for v in vectors],
        ],
        out_shape=[
            jax.ShapeDtypeStruct((rows, width), BF16),
            out(rows, width),
            out(768, width),
            out(768, width),
            out(3, 192, width),
            out(192, width),
            out(2, 3, HD, HD),
            out(3, 192),
            out(3, 2, HD),
            *[out(*v) for v in vectors],
        ],
        name="finish",
    )(res, tok, outer, inner, early, early, late, late, small)


def shards(
    fast,
    tokens,
    first_gain,
    first_bias,
    mixer_weight,
    mixer_bias,
    feature_weight,
    feature_bias,
    output_weight,
    output_bias,
    second_gain,
    second_bias,
    inner_weight,
    inner_bias,
    outer_weight,
    outer_bias,
    block_owner,
    cotangent,
):
    rows, width = tokens.shape
    n_tp, n_ctx = lax.axis_size("tp"), lax.axis_size("ctx")
    n_plane = lax.axis_size("dp") * n_ctx
    plane = lax.axis_index("dp") * n_ctx + lax.axis_index("ctx")
    heads_here = mixer_weight.shape[2] // HD
    heads = heads_here * n_tp
    mine = lax.axis_index("ctx") * n_tp + lax.axis_index("tp")

    mixer_t = mixer_weight.transpose(1, 2, 0).reshape(-1, width)
    if fast:
        vectors = (
            first_gain, first_bias, output_bias, second_gain, second_bias, outer_bias, inner_bias
        )
        raw = block_call(
            tokens,
            cotangent,
            mixer_t,
            output_weight,
            inner_weight,
            outer_weight,
            feature_weight,
            mixer_bias,
            feature_bias.transpose(1, 0, 2),
            *[v.reshape(6, 128) for v in vectors],
        )
        (
            result, tokens_gradient, d_outer, d_inner, d_mixer, d_output,
            d_feature, d_mixer_bias, d_feature_bias, *shared
        ) = finish_call(*raw)
        shared = [v.reshape(width) for v in shared]
        return (
            result,
            tokens_gradient,
            shared[0],
            shared[1],
            d_mixer.transpose(2, 0, 1),
            d_mixer_bias,
            d_feature,
            d_feature_bias.transpose(1, 0, 2),
            d_output,
            shared[2],
            shared[3],
            shared[4],
            d_inner,
            shared[6],
            d_outer,
            shared[5],
        )
    sizes = [w.shape[0] for w in (mixer_t, output_weight, inner_weight, outer_weight)]
    pack = jnp.concatenate([mixer_t, output_weight, inner_weight, outer_weight], axis=0)
    part = pack.shape[0] // n_plane
    piece = lax.dynamic_slice_in_dim(pack, plane * part, part, 0)
    full = lax.all_gather(piece, ALL, axis=0, tiled=True)
    full = full.reshape(n_plane, n_tp, part, width).transpose(1, 0, 2, 3).reshape(n_tp, -1, width)
    cuts = [0]
    for s in sizes:
        cuts.append(cuts[-1] + s)
    mixer_all, output_all, inner_all, outer_all = [
        full[:, a:b] for a, b in zip(cuts[:-1], cuts[1:])
    ]
    small = jnp.concatenate(
        [feature_weight.reshape(-1), mixer_bias.reshape(-1), feature_bias.reshape(-1), inner_bias]
    )
    small = lax.all_gather(small, "tp")
    cut = feature_weight.size
    feature_all = (
        small[:, :cut].reshape(n_tp, 2, heads_here, HD, HD).transpose(1, 0, 2, 3, 4)
    ).reshape(2, heads, HD, HD)
    mixer_bias_all = small[:, cut : cut + mixer_bias.size].astype(F32).reshape(n_tp, -1)
    cut += mixer_bias.size
    feature_bias_all = (
        small[:, cut : cut + feature_bias.size]
        .astype(F32)
        .reshape(n_tp, 2, heads_here, HD)
        .transpose(1, 0, 2, 3)
        .reshape(2, heads, HD)
    )
    cut += feature_bias.size
    inner_bias_all = small[:, cut:].astype(F32)

    x = tokens.astype(F32)
    gain1, gain2 = first_gain.astype(F32), second_gain.astype(F32)
    h1, n1, r1 = layer_norm(x, gain1, first_bias.astype(F32))
    h1 = h1.astype(BF16)
    mix = ein("td,skd->tsk", h1, mixer_all) + mixer_bias_all
    mix = mix.astype(BF16).reshape(rows, n_tp, 3, heads_here, HD).transpose(2, 0, 1, 3, 4)
    mix = mix.reshape(3, rows, heads, HD)
    q, k, v = mix[0], mix[1], mix[2]
    q_up, q_down, phi_q = feature_map(q, feature_all[0], feature_bias_all[0])
    k_up, k_down, phi_k = feature_map(k, feature_all[1], feature_bias_all[1])

    chunk = min(CHUNK, rows)
    chunks = rows // chunk
    pq = phi_q.reshape(chunks, chunk, heads, 2 * HD)
    pk = phi_k.reshape(chunks, chunk, heads, 2 * HD)
    vc = v.reshape(chunks, chunk, heads, HD)
    causal = jnp.arange(chunk)[:, None] >= jnp.arange(chunk)[None, :]
    state = ein("jthe,jthf->jhef", vc, pk)
    norm = jnp.sum(pk.astype(F32), axis=1)
    both = jnp.concatenate([state, norm[:, :, None]], axis=2)
    owners = block_owner[0].reshape(n_tp, -1)[:, 0]
    order = jnp.arange(n_ctx * n_tp)
    same = jnp.tile(owners, n_ctx) == jnp.tile(owners, n_ctx)[mine]

    def prefix(totals, reach):
        everything = lax.all_gather(totals.astype(BF16), ("ctx", "tp")).astype(F32)
        return jnp.einsum("s,shef->hef", reach.astype(F32), everything, precision="highest")

    def running(blocks, start, reverse):
        out = [None] * chunks
        acc = start
        for j in reversed(range(chunks)) if reverse else range(chunks):
            out[j] = acc
            acc = acc + blocks[j]
        return jnp.stack(out)

    before = running(both, prefix(jnp.sum(both, axis=0), same & (order < mine)), False)
    before = before.astype(BF16)
    scores = ein("jthf,jshf->jhts", pq, pk)
    a_low = jnp.where(causal, scores, 0.0).astype(BF16)
    v_one = jnp.concatenate([vc, jnp.ones(vc.shape[:-1] + (1,), BF16)], axis=-1)
    num = ein("jthf,jhef->jthe", pq, before) + ein("jhts,jshe->jthe", a_low, v_one)
    num, den = num[..., :HD], num[..., HD:]
    o = num / den
    o_low = o.astype(BF16)
    o_flat = o_low.reshape(rows, n_tp, heads_here * HD)
    x2 = x + ein("tsk,skd->td", o_flat, output_all) + output_bias.astype(F32)
    h2, n2, r2 = layer_norm(x2, gain2, second_bias.astype(F32))
    h2 = h2.astype(BF16)
    f = ein("td,sdf->tsf", h2, inner_all) + inner_bias_all
    a, slope = gelu_parts(f)
    a = a.astype(BF16)
    result = (x2 + ein("tsf,sfd->td", a, outer_all) + outer_bias.astype(F32)).astype(BF16)

    g = cotangent.astype(F32)
    d_outer = ein("tsf,td->sfd", a, cotangent)
    df = (ein("td,sfd->tsf", cotangent, outer_all) * slope).astype(BF16)
    d_inner_bias = jnp.sum(df.astype(F32), axis=0)
    d_inner = ein("td,tsf->sdf", h2, df)
    e2 = ein("tsf,sdf->td", df, inner_all)
    back2, d_gain2, d_bias2 = layer_norm_back(e2, n2, r2, gain2)
    dx2 = g + back2
    big_g = dx2.astype(BF16)
    d_output = ein("tsk,td->skd", o_flat, big_g)
    do = ein("td,skd->tsk", big_g, output_all).astype(BF16).astype(F32)
    do = do.reshape(chunks, chunk, heads, HD)
    dnum = do / den
    dden = -jnp.sum(do * o, axis=-1, keepdims=True) / den
    dne = jnp.concatenate([dnum, dden], axis=-1).astype(BF16)
    da = ein("jthe,jshe->jhts", dne, v_one)
    da_low = jnp.where(causal, da, 0.0).astype(BF16)
    d_both = ein("jthe,jthf->jhef", dne, pq)
    after = running(d_both, prefix(jnp.sum(d_both, axis=0), same & (order > mine)), True)
    after = after.astype(BF16)
    dphi_q = ein("jhts,jshf->jthf", da_low, pk) + ein("jthe,jhef->jthf", dne, before)
    dphi_k = ein("jhts,jthf->jshf", da_low, pq) + ein("jthe,jhef->jthf", v_one, after)
    dv = ein("jhts,jthe->jshe", a_low, dne[..., :HD]) + ein("jthf,jhef->jthe", pk, after[:, :, :HD])
    dphi_q = dphi_q.reshape(rows, heads, 2 * HD)
    dphi_k = dphi_k.reshape(rows, heads, 2 * HD)
    dq, d_fq, d_fbq = feature_back(dphi_q, q_up, q_down, q, feature_all[0])
    dk, d_fk, d_fbk = feature_back(dphi_k, k_up, k_down, k, feature_all[1])
    dmix = jnp.stack([dq, dk, dv.reshape(rows, heads, HD)], axis=1).astype(BF16)
    dmix = dmix.reshape(rows, 3, n_tp, heads_here * HD).transpose(0, 2, 1, 3)
    dmix = dmix.reshape(rows, n_tp, -1)
    d_mixer_bias = jnp.sum(dmix.astype(F32), axis=0)
    d_mixer = ein("tsk,td->skd", dmix, h1)
    e1 = ein("tsk,skd->td", dmix, mixer_all)
    back1, d_gain1, d_bias1 = layer_norm_back(e1, n1, r1, gain1)
    tokens_gradient = dx2 + back1

    big = jnp.concatenate([d_mixer, d_output, d_inner, d_outer], axis=1).astype(BF16)
    big = big.reshape(n_tp, n_plane, part, width).transpose(1, 0, 2, 3).reshape(-1, width)
    big = lax.psum_scatter(big, ("dp", "ctx"), scatter_dimension=0, tiled=True)
    big = lax.psum_scatter(big, "tp", scatter_dimension=0, tiled=True)
    big = lax.all_gather(big, ("dp", "ctx"), axis=0, tiled=True).astype(F32)
    d_mixer, d_output, d_inner, d_outer = [big[a:b] for a, b in zip(cuts[:-1], cuts[1:])]
    d_mixer = d_mixer.reshape(3, heads_here * HD, width).transpose(2, 0, 1)
    per_tp = jnp.concatenate(
        [
            jnp.stack([d_fq, d_fk]).reshape(2, n_tp, -1).transpose(1, 0, 2).reshape(n_tp, -1),
            d_mixer_bias,
            jnp.stack([d_fbq, d_fbk]).reshape(2, n_tp, -1).transpose(1, 0, 2).reshape(n_tp, -1),
            d_inner_bias,
        ],
        axis=1,
    )
    shared = jnp.stack(
        [d_gain1, d_bias1, jnp.sum(dx2, axis=0), d_gain2, d_bias2, jnp.sum(g, axis=0)]
    )
    total = lax.psum(jnp.concatenate([per_tp.reshape(-1), shared.reshape(-1)]), ALL)
    shared = total[per_tp.size :].reshape(6, width)
    own = lax.dynamic_slice_in_dim(
        total[: per_tp.size].reshape(n_tp, -1), lax.axis_index("tp"), 1, 0
    )[0]
    cut = feature_weight.size
    d_feature = own[:cut].reshape(feature_weight.shape)
    d_mixer_bias = own[cut : cut + mixer_bias.size].reshape(mixer_bias.shape)
    cut += mixer_bias.size
    d_feature_bias = own[cut : cut + feature_bias.size].reshape(feature_bias.shape)
    d_inner_bias = own[cut + feature_bias.size :]
    return (
        result,
        tokens_gradient,
        shared[0],
        shared[1],
        d_mixer,
        d_mixer_bias,
        d_feature,
        d_feature_bias,
        d_output,
        shared[2],
        shared[3],
        shared[4],
        d_inner,
        d_inner_bias,
        d_outer,
        shared[5],
    )


def solution(mesh):
    in_specs = (
        P(("dp", "ctx", "tp"), None),
        P(),
        P(),
        P(None, None, "tp"),
        P(None, "tp"),
        P(None, "tp", None, None),
        P(None, "tp", None),
        P("tp", None),
        P(),
        P(),
        P(),
        P(None, "tp"),
        P("tp"),
        P("tp", None),
        P(),
        P("dp", None),
        P(("dp", "ctx", "tp"), None),
    )
    out_specs = (
        P(("dp", "ctx", "tp"), None),
        P(("dp", "ctx", "tp"), None),
        P(),
        P(),
        P(None, None, "tp"),
        P(None, "tp"),
        P(None, "tp", None, None),
        P(None, "tp", None),
        P("tp", None),
        P(),
        P(),
        P(),
        P(None, "tp"),
        P("tp"),
        P("tp", None),
        P(),
    )
    fast = (mesh.shape["dp"], mesh.shape["ctx"], mesh.shape["tp"]) == (2, 4, 4)
    return jax.shard_map(functools.partial(shards, fast), mesh=mesh, in_specs=in_specs, out_specs=out_specs, check_vma=False)
```

profile of v0, /device:TPU:0, one launch (start us, length us, event | category | flops | bytes accessed | tf_op | source)
XLA Modules:
  0.0 181.4 jit_solution(5201674077239910909)
XLA Ops:
  0.7 173.5 %block.1 = (bf16[512,768]{1,0:T(8,128)(2,1)}, f32[512,768]{1,0:T(8,128)}, bf16[768,768]{1,0:T(8,128)(2,1)}, bf16[768,768]{1,0:T(8,128)(2,1)}, bf16[384,768]{1,0:...) custom-call(bf16[512,768]{1,0:T(8,128)(2,1)} %x.1, bf16[512,768]{1,0:T(8,128)(2,1)} %g.1, ...), custom_call_target="tpu_custom_call" | custom-call | tf_op jit(solution)/shard_map/block/pallas_call | solution.py:1191
  174.2 7.0 %finish.1 = (bf16[512,768]{1,0:T(8,128)(2,1)}, f32[512,768]{1,0:T(8,128)}, f32[768,768]{1,0:T(8,128)}, f32[768,768]{1,0:T(8,128)}, f32[3,192,768]{2,1,0:T(8,128)...) custom-call(bf16[512,768]{1,0:T(8,128)(2,1)} %get-tuple-element.39.r, ...), custom_call_target="tpu_custom_call" | custom-call | tf_op jit(solution)/shard_map/finish/pallas_call | solution.py:1246
where the time goes:
time: 182 us; the launch traced here: 181 us
  Pallas kernels  181 us (99%)
    pallas_call x1, Pallas kernels, block_call(): pl.pallas_call(body, out_shape=results, in_specs=[anywhere] * len(args),...  174 us
    pallas_call x1, Pallas kernels, finish_call(): pl.pallas_call(finish_kernel, grid=(steps,), in_specs=[spec(rows // steps...  7.01 us

commit v1 on v0

--- a/solution.py
+++ b/solution.py
@@ -813,28 +813,28 @@
         hand(1, k, lambda core: dot(H2[...], DF[slot, :, lanes(core)], 0, 0))
 
     m.DIB[...] = jnp.zeros_like(m.DIB)
-    order = [0] + K
+    order = K + [0]
     loads[5].wait()
     for g in both:
         g.diag(K[0])
-        g.xy(K[1])
     hidden(t0, 0)
     for g in both:
-        g.xy(K[2])
-        g.diag(K[1])
-    hand_hidden(0, 0)
+        g.xy(K[1])
     for n, k in enumerate(K):
         g1.done(k)
         g2.done(k)
-        hidden(shard(k), n // 2)
-        if n == 0:
-            for g in both:
+        hidden(shard(k), 1)
+        for g in both:
+            if n == 0:
+                g.xy(K[2])
+                g.diag(K[1])
+            if n == 1:
                 g.diag(K[2])
+        if n:
+            meet(1, K[n - 1])
         if n < 2:
-            for i in range(2):
-                meet(i, order[n])
-        if n < 1:
-            hand_hidden(k, 0)
+            hand_hidden(k, 1)
+            meet(0, k)
     for g in both:
         g.drain(True)
     RES, GG = W1.at[2, pl.ds(0, 512)], W1.at[3, pl.ds(0, 512)]
@@ -890,12 +890,12 @@
         scan.begin(t)
 
     loop(4, give)
-    hand(0, order[2], lambda core: dot(A[0], CT[:, lanes(core)], 0, 0))
+    hand(0, order[2], lambda core: dot(A[1], CT[:, lanes(core)], 0, 0))
     for g in range(4):
         scan.pair(g)
     for i in range(2):
         R[i].two(order[0])
-    hand(1, order[2], lambda core: dot(H2[...], DF[0, :, lanes(core)], 0, 0))
+    hand(1, order[2], lambda core: dot(H2[...], DF[1, :, lanes(core)], 0, 0))
     for i in range(2):
         R[i].two(order[1])
 
@@ -961,29 +961,28 @@
     for i in range(2):
         meet(i, order[2])
     loop(2, lambda g: ask(g + 2))
+    hand_hidden(0, 0)
+    for g in range(4):
+        scan.relay(g)
     for i in range(2):
         R[i].three(order[0])
         R[i].three(order[1])
-    for g in range(4):
-        scan.relay(g)
-    hand_hidden(order[3], 1)
     RES[...] = ACC_O[...].astype(BF16)
     res_copy = pltpu.make_async_copy(RES, m.result, ld.at[6])
     res_copy.start()
+    early(order[0])
+    for i in range(2):
+        meet(i, order[3])
+    early(order[1])
+    meet(2, order[0])
     for i in range(2):
         R[i].two(order[2])
-        meet(i, order[3])
-    early(order[0])
-    early(order[1])
-    meet(2, order[0])
-    R[0].three(order[2])
     early(order[2])
     meet(2, order[1])
-    R[1].three(order[2])
+    early(order[3])
+    meet(2, order[2])
     for i in range(2):
         R[i].two(order[3])
-    early(order[3])
-    meet(2, order[2])
     enter(1)
 
     def key_back(t, i):
@@ -1011,6 +1010,8 @@
         loop(3, lambda i: key_back(t, i))
         hand(3, k, lambda core: dot(MIX[t, 192:576], H1[:, lanes(core)], 1, 0))
         if n == 0:
+            for i in range(2):
+                R[i].three(order[2])
             meet(2, order[3])
             R[2].two(order[0])
             R[2].two(order[1])
@@ -1024,9 +1025,11 @@
             R[2].two(order[3])
             R[2].three(order[0])
             R[2].three(order[1])
+            R[3].two(order[0])
+            R[0].final()
+            R[1].final()
+        if n == 3:
             R[2].three(order[2])
-            R[3].two(order[0])
-        if n == 3:
             R[2].three(order[3])
             R[3].two(order[1])
             R[3].three(order[0])
@@ -1043,12 +1046,13 @@
 
     back1(0)
     meet(3, order[3])
+    R[0].spread()
     R[3].two(order[2])
-    R[0].final()
+    R[1].spread()
     R[3].three(order[1])
-    R[1].final()
     back1(1)
-    R[0].spread()
+    R[3].two(order[3])
+    R[0].corner()
     tok_copy = pltpu.make_async_copy(ACC_E, m.tokens_gradient, ld.at[7])
     tok_copy.start()
     for k in range(6):
@@ -1065,13 +1069,10 @@
         GB[:, 128 * t : 128 * t + 128] = GS[t].astype(BF16)
     tiny = Small(p, GB, GS, m.plane, m.line, m.mid, m.outs[4], m.small_sems, m.small_send, m.own.at[4])
     tiny.begin()
-    R[3].two(order[3])
-    R[1].spread()
+    R[2].final()
     R[3].three(order[2])
-    R[2].final()
-    R[0].corner()
+    R[1].corner()
     R[3].three(order[3])
-    R[1].corner()
     tiny.across()
     R[2].spread()
     R[3].final()

time: 182 us -> 176 us (0.967)
  Pallas kernels: 181 us -> 174 us
    pallas_call x1, Pallas kernels: 174 us -> 167 us  [block_call(): pl.pallas_call(body, out_shape=results, in_specs=[anywhere] * len(args),...]
where the time goes in v1:
time: 176 us; the launch traced here: 175 us
  Pallas kernels  174 us (99%)
    pallas_call x1, Pallas kernels, block_call(): pl.pallas_call(body, out_shape=results, in_specs=[anywhere] * len(args),...  167 us
    pallas_call x1, Pallas kernels, finish_call(): pl.pallas_call(finish_kernel, grid=(steps,), in_specs=[spec(rows // steps...  7.01 us

profile of v1, /device:TPU:0, one launch (start us, length us, event | category | flops | bytes accessed | tf_op | source)
XLA Modules:
  0.0 175.1 jit_solution(123394761696584959)
XLA Ops:
  0.7 167.2 %block.1 = (bf16[512,768]{1,0:T(8,128)(2,1)}, f32[512,768]{1,0:T(8,128)}, bf16[768,768]{1,0:T(8,128)(2,1)}, bf16[768,768]{1,0:T(8,128)(2,1)}, bf16[384,768]{1,0:...) custom-call(bf16[512,768]{1,0:T(8,128)(2,1)} %x.1, bf16[512,768]{1,0:T(8,128)(2,1)} %g.1, ...), custom_call_target="tpu_custom_call" | custom-call | tf_op jit(solution)/shard_map/block/pallas_call | solution.py:1192
  167.9 7.0 %finish.1 = (bf16[512,768]{1,0:T(8,128)(2,1)}, f32[512,768]{1,0:T(8,128)}, f32[768,768]{1,0:T(8,128)}, f32[768,768]{1,0:T(8,128)}, f32[3,192,768]{2,1,0:T(8,128)...) custom-call(bf16[512,768]{1,0:T(8,128)(2,1)} %get-tuple-element.39.r, ...), custom_call_target="tpu_custom_call" | custom-call | tf_op jit(solution)/shard_map/finish/pallas_call | solution.py:1247

commit v2 on v1

--- a/solution.py
+++ b/solution.py
@@ -143,17 +143,22 @@
 
 
 class Gather:
-    def __init__(self, p, buf, sems, send, index):
+    def __init__(self, p, buf, sems, send, index, base=0, rows=None):
         self.p, self.buf, self.sems, self.send, self.i = p, buf, sems, send.at[index], index
-        self.rows = buf.shape[1]
-        self.piece = self.rows // 8
-        self.half = self.piece // 2
+        self.base, self.rows = base, rows or buf.shape[1]
+        self.wide = buf.shape[2] == 768
+        self.piece = self.rows // (4 if self.wide else 8)
+        self.lanes = lanes(0) if self.wide else slice(None)
+
     def at(self, t, q, core, half=None):
-        start = q * (2 * self.piece) + core * self.piece
+        start = q * (self.rows // 4) + (0 if self.wide else core * self.piece)
         size = self.piece
         if half is not None:
-            start, size = start + half * self.half, self.half
-        return self.buf.at[t, pl.ds(pl.multiple_of(start, 16), size)]
+            first = (size + 16) // 32 * 16
+            start, size = start + half * first, size - first if half else first
+        rows = pl.ds(pl.multiple_of(self.base + start, 16), size)
+        return self.buf.at[t, rows, lanes(core)] if self.wide else self.buf.at[t, rows]
+
     def shard(self, k): return lax.rem(self.p.t + k, 4)
     def copy(self, ref, kind, k, peer):
         n = 0 if kind == "z" else 2 if kind == "c" else 1
@@ -207,27 +212,34 @@
         p, t = self.p, self.shard(k)
         self.copy(self.at(t, p.qd, p.core, 0), "fy", k, p.y_nb).wait_recv()
         self.copy(self.at(t, p.qd, p.core, 1), "fx", k, p.x_nb).wait_recv()
-        for q in range(4):
-            self.go(self.at(t, q, p.core), "c", k, p.core_nb)
+        if self.wide:
+            self.go(self.buf.at[t, pl.ds(self.base, self.rows), lanes(p.core)], "c", k, p.core_nb)
+        else:
+            for q in range(4):
+                self.go(self.at(t, q, p.core), "c", k, p.core_nb)
+
     def done(self, k):
         p, t = self.p, self.shard(k)
-        self.copy(self.buf.at[t, pl.ds(0, 4 * self.piece)], "c", k, p.core_nb).wait_recv()
+        if self.wide:
+            ref = self.buf.at[t, pl.ds(self.base, self.rows), lanes(1 - p.core)]
+        else:
+            ref = self.buf.at[t, pl.ds(0, 4 * self.piece)]
+        self.copy(ref, "c", k, p.core_nb).wait_recv()
 
     def drain(self, hops):
-        p = self.p
+        p, n = self.p, self.piece
 
         def wait(kind, ref):
             self.copy(ref, kind, 1, p.core_nb).wait_send()
 
-        line = lambda n: wait("z", self.buf.at[0, pl.ds(0, n * self.piece)])
         if hops:
             ends = jnp.logical_or(p.t == 0, p.t == 3)
-            pl.when(ends)(lambda: line(1))
-            pl.when(jnp.logical_not(ends))(lambda: line(5))
+            pl.when(ends)(lambda: wait("z", self.buf.at[0, pl.ds(0, n // 2)]))
+            pl.when(jnp.logical_not(ends))(lambda: wait("z", self.buf.at[0, pl.ds(0, 5 * n // 2)]))
         else:
-            line(3)
-        wait("x", self.buf.at[pl.ds(0, 3), pl.ds(0, 3 * self.piece)])
-        wait("c", self.buf.at[pl.ds(0, 3), pl.ds(0, 4 * self.piece)])
+            wait("z", self.buf.at[0, pl.ds(0, 3 * n), self.lanes])
+        wait("x", self.buf.at[pl.ds(0, 3), pl.ds(0, 3 * n), self.lanes])
+        wait("c", self.buf.at[pl.ds(0, 3), pl.ds(0, 4 * n), self.lanes])
 
 
 def lanes(core):
@@ -582,13 +594,14 @@
         for i in range(6):
             VEC[k : k + 1, 128 * i : 128 * i + 128] = value[i : i + 1]
 
-    gs, gw, g1, g2 = gathers = [
-        Gather(p, b, m.gather_sems, m.gather_send, i) for i, b in enumerate((S, WA, W1, W2))
+    packs = ((S, 0, 256), (WA, 0, 576), (W1, 0, 768), (W2, 0, 768), (WA, 576, 192))
+    gs, gw, g1, g2, go = [
+        Gather(p, buf, m.gather_sems, m.gather_send, i, base, rows)
+        for i, (buf, base, rows) in enumerate(packs)
     ]
     K = nearest(t0)
     shard = gs.shard
     loads[0].wait()
-    loads[1].wait()
     met(p)
     gw.first()
     gs.first()
@@ -659,8 +672,9 @@
         gw.z(k)
         gs.z(k)
         if n == 1:
-            loads[3].wait()
-            loads[4].wait()
+            for c in (loads[1], loads[3], loads[4]):
+                c.wait()
+            go.first()
             for g in both:
                 g.first_hop()
     for k in K:
@@ -670,6 +684,8 @@
         gw.diag(k)
         gs.diag(k)
     middle = jnp.logical_or(t0 == 1, t0 == 2)
+    for k in K:
+        go.z(k)
     for g in both:
         g.zf(K[0])
         g.spread(K[0])
@@ -699,6 +715,8 @@
             a = dot(PH[1, h, :, c], PH[0, h, :, c], 0, 0)
             AT[h, j] = jnp.where(causal, a, 0.0).astype(BF16)
 
+    for k in K:
+        go.xy(k)
     for g in both:
         g.zf(jnp.where(middle, K[2], K[1]))
     for g in range(4):
@@ -706,6 +724,8 @@
     loop(12, scores)
     for g in range(4):
         scan.chain(g)
+    for k in K:
+        go.diag(k)
     for g in both:
         g.xy(K[0])
         g.spread(K[1])
@@ -735,6 +755,8 @@
             OT[ds(h, 64), c] = (num[0:64] * r).astype(BF16)
 
     loop(12, attend)
+    for k in K:
+        go.done(k)
 
     def norm2(i):
         r = ds(i, 256)
@@ -1088,6 +1110,7 @@
         c.wait_send()
     gs.drain(False)
     gw.drain(False)
+    go.drain(False)
     res_copy.wait()
     tok_copy.wait()
 
@@ -1156,8 +1179,8 @@
         ld=dma((18,)),
         own=dma((5,)),
         r_core=dma((2, 4, 4)),
-        gather_sems={k: dma((4, 3)) for k in GATHER_SEMS},
-        gather_send=dma((4, 3)),
+        gather_sems={k: dma((5, 3)) for k in GATHER_SEMS},
+        gather_send=dma((5, 3)),
         reduce_sems={k: dma((4, n)) for k, n in zip(SEMS, (4, 4, 4, 4, 3, 5))},
         reduce_send=dma((4, 4)),
         small_sems=dma((17,)),

time: 176 us -> 171 us (0.972)
  Pallas kernels: 174 us -> 169 us
    pallas_call x1, Pallas kernels: 167 us -> 162 us  [block_call(): pl.pallas_call(body, out_shape=results, in_specs=[anywhere] * len(args),...]
where the time goes in v2:
time: 171 us; the launch traced here: 170 us
  Pallas kernels  169 us (99%)
    pallas_call x1, Pallas kernels, block_call(): pl.pallas_call(body, out_shape=results, in_specs=[anywhere] * len(args),...  162 us
    pallas_call x1, Pallas kernels, finish_call(): pl.pallas_call(finish_kernel, grid=(steps,), in_specs=[spec(rows // steps...  7.01 us

profile of v2, /device:TPU:0, one launch (start us, length us, event | category | flops | bytes accessed | tf_op | source)
XLA Modules:
  0.0 170.0 jit_solution(16271896915730961560)
XLA Ops:
  0.7 162.1 %block.1 = (bf16[512,768]{1,0:T(8,128)(2,1)}, f32[512,768]{1,0:T(8,128)}, bf16[768,768]{1,0:T(8,128)(2,1)}, bf16[768,768]{1,0:T(8,128)(2,1)}, bf16[384,768]{1,0:...) custom-call(bf16[512,768]{1,0:T(8,128)(2,1)} %x.1, bf16[512,768]{1,0:T(8,128)(2,1)} %g.1, ...), custom_call_target="tpu_custom_call" | custom-call | tf_op jit(solution)/shard_map/block/pallas_call | solution.py:1215
  162.7 7.0 %finish.1 = (bf16[512,768]{1,0:T(8,128)(2,1)}, f32[512,768]{1,0:T(8,128)}, f32[768,768]{1,0:T(8,128)}, f32[768,768]{1,0:T(8,128)}, f32[3,192,768]{2,1,0:T(8,128)...) custom-call(bf16[512,768]{1,0:T(8,128)(2,1)} %get-tuple-element.39.r, ...), custom_call_target="tpu_custom_call" | custom-call | tf_op jit(solution)/shard_map/finish/pallas_call | solution.py:1270

commit v3 on v2

--- a/solution.py
+++ b/solution.py
@@ -842,6 +842,7 @@
     hidden(t0, 0)
     for g in both:
         g.xy(K[1])
+    hand(0, 0, lambda core: dot(A[0], CT[:, lanes(core)], 0, 0))
     for n, k in enumerate(K):
         g1.done(k)
         g2.done(k)
@@ -854,6 +855,8 @@
                 g.diag(K[2])
         if n:
             meet(1, K[n - 1])
+        else:
+            meet(0, 0)
         if n < 2:
             hand_hidden(k, 1)
             meet(0, k)
@@ -915,6 +918,7 @@
     hand(0, order[2], lambda core: dot(A[1], CT[:, lanes(core)], 0, 0))
     for g in range(4):
         scan.pair(g)
+    R[0].two(0)
     for i in range(2):
         R[i].two(order[0])
     hand(1, order[2], lambda core: dot(H2[...], DF[1, :, lanes(core)], 0, 0))
@@ -983,9 +987,10 @@
     for i in range(2):
         meet(i, order[2])
     loop(2, lambda g: ask(g + 2))
-    hand_hidden(0, 0)
+    hand(1, 0, lambda core: dot(H2[...], DF[0, :, lanes(core)], 0, 0))
     for g in range(4):
         scan.relay(g)
+    R[0].three(0)
     for i in range(2):
         R[i].three(order[0])
         R[i].three(order[1])
@@ -993,8 +998,7 @@
     res_copy = pltpu.make_async_copy(RES, m.result, ld.at[6])
     res_copy.start()
     early(order[0])
-    for i in range(2):
-        meet(i, order[3])
+    meet(1, order[3])
     early(order[1])
     meet(2, order[0])
     for i in range(2):
@@ -1003,8 +1007,7 @@
     meet(2, order[1])
     early(order[3])
     meet(2, order[2])
-    for i in range(2):
-        R[i].two(order[3])
+    R[1].two(order[3])
     enter(1)
 
     def key_back(t, i):
@@ -1040,7 +1043,6 @@
         else:
             meet(3, order[n - 1])
         if n == 1:
-            R[0].three(order[3])
             R[1].three(order[3])
             R[2].two(order[2])
         if n == 2:

time: 171 us -> 171 us (level)
  no operation moved by 1% of the time
where the time goes in v3:
time: 171 us
  Pallas kernels  170 us (99%)
    pallas_call x1, Pallas kernels, block_call(): pl.pallas_call(body, out_shape=results, in_specs=[anywhere] * len(args),...  163 us
    pallas_call x1, Pallas kernels, finish_call(): pl.pallas_call(finish_kernel, grid=(steps,), in_specs=[spec(rows // steps...  7.01 us

profile of v3, /device:TPU:0, one launch (start us, length us, event | category | flops | bytes accessed | tf_op | source)
XLA Modules:
  0.0 170.9 jit_solution(8646466329151881452)
XLA Ops:
  0.7 163.0 %block.1 = (bf16[512,768]{1,0:T(8,128)(2,1)}, f32[512,768]{1,0:T(8,128)}, bf16[768,768]{1,0:T(8,128)(2,1)}, bf16[768,768]{1,0:T(8,128)(2,1)}, bf16[384,768]{1,0:...) custom-call(bf16[512,768]{1,0:T(8,128)(2,1)} %x.1, bf16[512,768]{1,0:T(8,128)(2,1)} %g.1, ...), custom_call_target="tpu_custom_call" | custom-call | tf_op jit(solution)/shard_map/block/pallas_call | solution.py:1217
  163.7 7.0 %finish.1 = (bf16[512,768]{1,0:T(8,128)(2,1)}, f32[512,768]{1,0:T(8,128)}, f32[768,768]{1,0:T(8,128)}, f32[768,768]{1,0:T(8,128)}, f32[3,192,768]{2,1,0:T(8,128)...) custom-call(bf16[512,768]{1,0:T(8,128)(2,1)} %get-tuple-element.39.r, ...), custom_call_target="tpu_custom_call" | custom-call | tf_op jit(solution)/shard_map/finish/pallas_call | solution.py:1272
